TPU v7x, 32 devices: a whole 2x2x4 slice. The times are simulated.
32 devices in a mesh: grp: 2 (over y), slab: 4 (over z), head: 2 (over x), seq: 2 (over core).
Axes of the slice: x: 2, y: 2, z: 4, core: 2. Of those that a mesh axis runs over, the one named last changes fastest.
Arguments:
- queries: bfloat16 [1024, 5120], P(('grp', 'seq'), 'head'), parts along dimension 0, may hold values from -140 to 140
- query_gain: float32 [5120], P('head'), may hold values from 1.5 to 3
- cache_keys: bfloat16 [4096, 5120], P(('grp', 'slab'), 'head'), parts along dimension 0, may hold values from -120 to 120
- cache_values: bfloat16 [4096, 5120], P(('grp', 'slab'), 'head'), parts along dimension 0, may hold values from -6 to 6
- finished_keys: bfloat16 [1024, 5120], P(('grp', 'slab', 'seq'), 'head'), parts along dimension 0, may hold values from -6 to 6
- finished_values: bfloat16 [1024, 5120], P(('grp', 'slab', 'seq'), 'head'), parts along dimension 0, may hold values from -6 to 6
- new_keys: bfloat16 [1024, 5120], P(('grp', 'slab', 'seq'), 'head'), parts along dimension 0, may hold values from -6 to 6
- new_values: bfloat16 [1024, 5120], P(('grp', 'slab', 'seq'), 'head'), parts along dimension 0, may hold values from -6 to 6
- out_weight: bfloat16 [5120, 5120], P('head', 'slab'), may hold values from -0.25 to 0.25
- time_weight: float32 [256, 5120], P(None, ('slab', 'head')), may hold values from -0.375 to 0.375
- owner: int32 [2], P('grp'), parts along dimension 0, may hold values from 0 to 3
- step: int32 [2], P('grp'), parts along dimension 0, may hold values from 0 to 999
Outputs:
- branch: bfloat16 [1024, 5120], P(('grp', 'seq'), ('slab', 'head')), parts along dimension 0
There are 2 independent parts, one for each index of `grp`. A program takes and returns all parts, laid end to end along the dimension named above; an argument that names none is the same for every part. Nothing has to cross between parts.
All inputs are finite; a program needn't handle non-finite values.
Results may differ from a plain program's by a relative error of at most 0.012.
Values may be sent and summed in bfloat16 or wider, within the bound.
No kernel may reach another device: no remote copies, remote signals or barrier semaphores. Data moves between devices by JAX's collectives and lax.ppermute only.
A program may use at most 64 MiB of HBM per device.

v0:
```python
from functools import reduce
import jax
import jax.numpy as jnp
from jax import lax
from jax.sharding import PartitionSpec as P

HEADS = 40
HD = 128
EPSILON = 1e-06


def local(
    queries,
    query_gain,
    cache_keys,
    cache_values,
    finished_keys,
    finished_values,
    new_keys,
    new_values,
    out_weight,
    time_weight,
    owner,
    step,
):
    row_count = queries.shape[0]
    head_count = queries.shape[1] // HD
    query_float = queries.astype(jnp.float32)
    norm_total = lax.psum(jnp.sum(query_float * query_float, axis=1), "head")
    inverse = lax.rsqrt(norm_total / (HEADS * HD) + EPSILON)
    normed = (
        (query_float * inverse[:, None] * query_gain)
        .astype(jnp.bfloat16)
        .reshape(row_count, head_count, HD)
    )
    is_owner = lax.axis_index("slab") == owner[0]
    whole_keys, whole_values = (
        lax.all_gather(finished_keys, ("slab", "seq"), axis=0, tiled=True),
        lax.all_gather(finished_values, ("slab", "seq"), axis=0, tiled=True),
    )
    fresh_keys, fresh_values = (
        lax.all_gather(new_keys, "seq", axis=0, tiled=True),
        lax.all_gather(new_values, "seq", axis=0, tiled=True),
    )
    key_block = jnp.where(is_owner, whole_keys, cache_keys)
    value_block = jnp.where(is_owner, whole_values, cache_values)
    blocks = [
        (key_block, value_block, jnp.float32(0.0)),
        (fresh_keys, fresh_values, jnp.float32(0.0)),
    ]
    score_scale = 1.0 / HD**0.5
    score_list = []
    for key_block, value_block, penalty in blocks:
        key_heads = key_block.reshape(key_block.shape[0], head_count, HD)
        each_score = jnp.einsum(
            "rhd,khd->hrk", normed, key_heads, preferred_element_type=jnp.float32
        )
        score_list.append(each_score * score_scale)
    row_top = reduce(jnp.maximum, [jnp.max(each_score, axis=2) for each_score in score_list])
    row_mass = jnp.zeros_like(row_top)
    partial_value = jnp.zeros((head_count, row_count, HD), jnp.float32)
    for each_score, (key_block, value_block, penalty) in zip(score_list, blocks):
        raw_weights = jnp.exp(each_score - row_top[:, :, None])
        row_mass = row_mass + jnp.sum(raw_weights, axis=2)
        value_heads = value_block.reshape(value_block.shape[0], head_count, HD)
        partial_value = partial_value + jnp.einsum(
            "hrk,khd->hrd",
            raw_weights.astype(jnp.bfloat16),
            value_heads,
            preferred_element_type=jnp.float32,
        )
    global_top = lax.pmax(row_top, "slab")
    factor = jnp.exp(row_top - global_top)
    sum_share, mass_share = (
        lax.psum_scatter(
            partial_value * factor[:, :, None], "slab", scatter_dimension=1, tiled=True
        ),
        lax.psum_scatter(row_mass * factor, "slab", scatter_dimension=1, tiled=True),
    )
    row_share = (sum_share / mass_share[:, :, None]).astype(jnp.bfloat16)
    attended = lax.all_gather(row_share, "slab", axis=1, tiled=True)
    weight_heads = out_weight.reshape(head_count, HD, out_weight.shape[1])
    projected = jnp.einsum(
        "hrd,hdc->rc", attended, weight_heads, preferred_element_type=jnp.float32
    )
    summed = lax.psum_scatter(projected, "head", scatter_dimension=1, tiled=True)
    half = time_weight.shape[0] // 2
    frequency = jnp.exp(-jnp.log(10000.0) * jnp.arange(half, dtype=jnp.float32) / half)
    phases = step[0].astype(jnp.float32) * frequency
    embedding = jnp.concatenate([jnp.cos(phases), jnp.sin(phases)])
    time_gate = 1.0 + jnp.dot(embedding, time_weight, precision=lax.Precision.HIGHEST)
    return (time_gate * summed).astype(jnp.bfloat16)


def solution(mesh):
    in_specs = (
        P(("grp", "seq"), "head"),
        P("head"),
        P(("grp", "slab"), "head"),
        P(("grp", "slab"), "head"),
        P(("grp", "slab", "seq"), "head"),
        P(("grp", "slab", "seq"), "head"),
        P(("grp", "slab", "seq"), "head"),
        P(("grp", "slab", "seq"), "head"),
        P("head", "slab"),
        P(None, ("slab", "head")),
        P("grp"),
        P("grp"),
    )
    out_specs = P(("grp", "seq"), ("slab", "head"))
    return jax.shard_map(local, mesh=mesh, in_specs=in_specs, out_specs=out_specs, check_vma=False)
```

profile of v0, /device:TPU:0, one launch (start us, length us, event | category | flops | bytes accessed | tf_op | source)
XLA Modules:
  0.0 240.0 jit_solution(8406601955525841598)
XLA Ops:
  6.5 0.7 all-gather.4.cloned.1.call-update
  7.3 0.0 all-gather.6.cloned.1.call-start
  7.3 0.7 all-gather.6.cloned.1.call-update
  8.0 0.0 reduce-scatter.10.cloned.1.call-start
  8.1 4.5 %copy.36 = bf16[512,2560]{0,1:T(8,128)(2,1)} copy(bf16[512,2560]{1,0:T(8,128)(2,1)} %param.15) | data formatting | bytes 5242880 | tf_op args[3]
  13.3 0.0 copy-done.3
  13.3 0.6 copy.27
  13.9 0.0 copy-start.4
  13.9 0.0 copy-start.5
  13.9 4.5 %copy.29 = bf16[512,2560]{0,1:T(8,128)(2,1)} copy(bf16[512,2560]{1,0:T(8,128)(2,1)} %param.14) | data formatting | bytes 5242880 | tf_op args[2]
  18.4 2.7 %all_gather.16 = bf16[128,2560]{1,0:T(8,128)(2,1)S(1)} all-gather(bf16[64,2560]{1,0:T(8,128)(2,1)S(1)} %copy-done.4), channel_id=1, replica_groups=mesh['grp'=2,'slab'=4,'head'=2,'seq'=2] {'seq'}, dimensions={0}, use_global_device_ids=true | all-gather | bytes 983040 | tf_op jit(solution)/shard_map/all_gather | solution.py:42
  21.1 1.1 copy.32
  22.2 2.3 all_gather.18
  24.4 1.1 copy.38
  25.5 0.4 fusion.6
  25.9 5.5 %psum.7 = f32[256]{0:T(256)S(1)} all-reduce(f32[256]{0:T(256)S(1)} %fusion.6), channel_id=1, replica_groups=mesh['grp'=2,'slab'=4,'head'=2,'seq'=2] {'head'}, use_global_device_ids=true, to_apply=%region_1.0 | all-reduce | flops 256 | bytes 2048 | tf_op jit(solution)/shard_map/psum | solution.py:29
  31.5 0.4 fusion.8
  31.9 1.2 copy-done.1
  33.0 1.7 multiply_reduce_fusion.1
  34.7 10.7 %all-gather.4.cloned.1.call-done = bf16[512,2560]{1,0:T(8,128)(2,1)} async-done(((bf16[64,2560]{1,0:T(8,128)(2,1)}), bf16[512,2560]{1,0:T(8,128)(2,1)}) %all-gather.4.cloned.1.call-update) | async-done | bytes 2621456 | tf_op jit(solution)/shard_map/all_gather | solution.py:38
  45.4 4.4 %copy.28 = bf16[512,2560]{0,1:T(8,128)(2,1)} copy(bf16[512,2560]{1,0:T(8,128)(2,1)} %all-gather.4.cloned.1.call-done) | data formatting | bytes 5242880 | tf_op jit(solution)/shard_map/all_gather | solution.py:38
  49.8 2.1 broadcast_select_fusion.1
  52.0 5.7 %multiply_reduce_fusion = (f32[20,256]{1,0:T(8,128)S(1)}, f32[20,256,512]{2,1,0:T(8,128)}) fusion(bf16[256,20,128]{0,2,1:T(8,128)(2,1)S(1)} %bitcast.25, bf16[512,20,128]{0,2,1:T(8,128)(2,1)S(1)} %bitcast.27), kind=kOutput, calls=%fused_computation.1 | convolution fusion | flops 676326400 | bytes 14438400 | tf_op jit(solution)/shard_map/rhd,khd->hrk/dot_general | solution.py:55
  57.6 18.7 %pmax.7 = f32[20,256]{1,0:T(8,128)S(1)} all-reduce(f32[20,256]{1,0:T(8,128)S(1)} %max.9), channel_id=1, replica_groups=mesh['grp'=2,'slab'=4,'head'=2,'seq'=2] {'slab'}, use_global_device_ids=true, to_apply=%region_4.5 | all-reduce | flops 5120 | bytes 40960 | tf_op jit(solution)/shard_map/pmax | solution.py:72
  76.4 5.9 %fusion = f32[20,256]{1,0:T(8,128)S(1)} fusion(f32[20,256,512]{2,1,0:T(8,128)} %get-tuple-element.8, f32[20,256]{1,0:T(8,128)S(1)} %max.9), kind=kLoop, calls=%fused_computation.2 | loop fusion | flops 7859200 | bytes 10526720 | tf_op jit(solution)/shard_map/reduce_sum | solution.py:64
  82.2 0.0 all-gather.6.cloned.1.call-done
  82.3 4.4 %copy.35 = bf16[512,2560]{0,1:T(8,128)(2,1)} copy(bf16[512,2560]{1,0:T(8,128)(2,1)} %all-gather.6.cloned.1.call-done) | data formatting | bytes 5242880 | tf_op jit(solution)/shard_map/all_gather | solution.py:39
  86.7 2.0 broadcast_select_fusion
  88.7 7.7 %fusion.2 = f32[20,256,128]{2,1,0:T(8,128)} fusion(bf16[512,20,128]{0,2,1:T(8,128)(2,1)S(1)} %bitcast.26, f32[20,256,512]{2,1,0:T(8,128)} %get-tuple-element.8, f32[20,256]{1,0:T(8,128)S(1)} %max.9), kind=kOutput, calls=%fused_computation.4 | convolution fusion | flops 678952960 | bytes 15749120 | tf_op jit(solution)/shard_map/hrk,khd->hrd/dot_general | solution.py:66
  96.4 0.5 fusion.9
  96.9 0.8 copy.48
  97.6 0.0 reduce-scatter.10.cloned.1.call-update
  97.7 0.0 reduce-scatter.6.cloned.1.call-start
  97.7 4.1 %add_multiply_fusion = f32[20,256,128]{2,1,0:T(8,128)} fusion(f32[20,256,128]{2,1,0:T(8,128)} %fusion.2, bf16[128,20,128]{0,2,1:T(8,128)(2,1)} %bitcast.28, f32[20,256,128]{1,2,0:T(8,128)S(1)} %get-tuple-element.10, f32[20,256]{1,0:T(8,128)S(1)} %get-tuple-element.6, f32[20,256]{1,0:T(8,128)S(1)} %max.9), kind=kOutput, calls=%fused_computation.13 | convolution fusion | flops 171048960 | bytes 8560640 | tf_op jit(solution)/shard_map/hrk,khd->hrd/dot_general | solution.py:66
  101.8 0.0 reduce-scatter.6.cloned.1.call-update
  101.8 0.0 all-gather.8.cloned.1.call-start
  101.9 13.7 %reduce-scatter.10.cloned.1.call-done = f32[64,20]{1,0:T(8,128)} async-done(((f32[256,20]{1,0:T(8,128)}), f32[64,20]{1,0:T(8,128)}) %reduce-scatter.10.cloned.1.call-update) | async-done | bytes 5136
  115.6 0.8 copy.49
  116.4 51.8 %reduce-scatter.6.cloned.1.call-done = f32[20,64,128]{2,1,0:T(8,128)} async-done(((f32[20,256,128]{2,1,0:T(8,128)}), f32[20,64,128]{2,1,0:T(8,128)}) %reduce-scatter.6.cloned.1.call-update) | async-done | bytes 655376 | tf_op jit(solution)/shard_map/reduce_scatter | solution.py:75
  168.2 2.1 divide_convert_fusion
  170.3 0.0 all-gather.8.cloned.1.call-update
  170.3 0.0 reduce-scatter.8.cloned.1.call-start
  170.4 32.2 %all-gather.8.cloned.1.call-done = bf16[20,256,128]{2,1,0:T(8,128)(2,1)} async-done(((bf16[20,64,128]{2,1,0:T(8,128)(2,1)}), bf16[20,256,128]{2,1,0:T(8,128)(2,1)}) %all-gather.8.cloned.1.call-update) | async-done | bytes 1310736 | tf_op jit(solution)/shard_map/all_gather | solution.py:81
  202.5 6.2 %convolution_bitcast_fusion = f32[256,1280]{1,0:T(8,128)} fusion(bf16[20,256,128]{2,1,0:T(8,128)(2,1)} %all-gather.8.cloned.1.call-done, bf16[20,128,1280]{2,1,0:T(8,128)(2,1)} %bitcast.33), kind=kOutput, calls=%fused_computation.9 | convolution fusion | flops 1677721600 | bytes 9175040 | tf_op jit(solution)/shard_map/hrd,hdc->rc/dot_general | solution.py:83
  208.7 0.0 reduce-scatter.8.cloned.1.call-update
  209.5 0.4 convolution_reduce_fusion
  209.9 21.4 %reduce-scatter.8.cloned.1.call-done = f32[256,640]{1,0:T(8,128)} async-done(((f32[256,1280]{1,0:T(8,128)}), f32[256,640]{1,0:T(8,128)}) %reduce-scatter.8.cloned.1.call-update) | async-done | bytes 655376 | tf_op jit(solution)/shard_map/reduce_scatter | solution.py:86
  231.3 1.9 multiply_convert_fusion
  (17 shorter events, 0.1 us)
Async XLA Ops:
  6.5 202.9 %copy-start = (f32[256,640]{1,0:T(8,128)S(1)}, f32[256,640]{1,0:T(8,128)}, u32[]{:S(2)}) copy-start(f32[256,640]{1,0:T(8,128)} %param.21) | copy-start | bytes 1966084
  6.5 38.9 %all-gather.4.cloned.1.call-start = ((), (), s32[]{:S(2)}) async-start(), calls=%async_computation.3 | async-start | bytes 2949120 | tf_op jit(solution)/shard_map/all_gather | solution.py:38
  7.3 75.0 %all-gather.6.cloned.1.call-start = ((), (), s32[]{:S(2)}) async-start(), calls=%async_computation.4 | async-start | bytes 2949120 | tf_op jit(solution)/shard_map/all_gather | solution.py:39
  8.0 107.6 %reduce-scatter.10.cloned.1.call-start = ((), (), s32[]{:S(2)}) async-start(), calls=%async_computation.8 | async-start | bytes 163840
  8.1 5.2 %copy-start.3 = (bf16[256,2560]{1,0:T(8,128)(2,1)S(1)}, bf16[256,2560]{1,0:T(8,128)(2,1)}, u32[]{:S(2)}) copy-start(bf16[256,2560]{1,0:T(8,128)(2,1)} %param.12) | copy-start | bytes 3932164
  13.9 4.5 %copy-start.4 = (bf16[64,2560]{1,0:T(8,128)(2,1)S(1)}, bf16[64,2560]{1,0:T(8,128)(2,1)}, u32[]{:S(2)}) copy-start(bf16[64,2560]{1,0:T(8,128)(2,1)} %param.18) | copy-start | bytes 983044
  13.9 8.3 %copy-start.5 = (bf16[64,2560]{1,0:T(8,128)(2,1)S(1)}, bf16[64,2560]{1,0:T(8,128)(2,1)}, u32[]{:S(2)}) copy-start(bf16[64,2560]{1,0:T(8,128)(2,1)} %param.19) | copy-start | bytes 983044
  21.1 10.4 %copy-start.6 = (f32[2560]{0:T(1024)S(1)}, f32[2560]{0:T(1024)}, u32[]{:S(2)}) copy-start(f32[2560]{0:T(1024)} %param.13) | copy-start | bytes 30724
  31.9 1.2 copy-start.1
  49.8 2.1 copy-start.2
  97.7 70.6 %reduce-scatter.6.cloned.1.call-start = ((), (), s32[]{:S(2)}) async-start(), calls=%async_computation.5 | async-start | bytes 3276800 | tf_op jit(solution)/shard_map/reduce_scatter | solution.py:75
  101.8 100.7 %all-gather.8.cloned.1.call-start = ((), (), s32[]{:S(2)}) async-start(), calls=%async_computation.6 | async-start | bytes 1638400 | tf_op jit(solution)/shard_map/all_gather | solution.py:81
  170.3 61.0 %reduce-scatter.8.cloned.1.call-start = ((), (), s32[]{:S(2)}) async-start(), calls=%async_computation.7 | async-start | bytes 1966080 | tf_op jit(solution)/shard_map/reduce_scatter | solution.py:86
Sparse Core Ops, SparseCore 0:
  9.0 36.4 all-gather.3
  47.1 33.8 all-gather.5
  97.8 17.7 reduce-scatter.9
  117.7 50.4 reduce-scatter.5
  170.4 32.0 all-gather.7
  208.9 22.3 reduce-scatter.7
where the time goes:
time: 241 us; the launch traced here: 240 us
  waiting for transfers between devices  131 us (54%)
  blocking collectives  29.2 us (12%)
  matrix products  25.7 us (11%)
  local copies, waits for them, and re-layouts  23.4 us (10%)
  other arithmetic  15.2 us (6%)
  between operations  14.9 us (6%)
    reduce_scatter x1, waiting for transfers between devices, local(): lax.psum_scatter(partial_value * factor[:, :, None], 'slab', scatter_dime...  51.8 us
    all_gather x1, waiting for transfers between devices, local(): attended = lax.all_gather(row_share, 'slab', axis=1, tiled=True)  32.2 us
    reduce_scatter x1, waiting for transfers between devices, local(): lax.psum_scatter(projected, 'head', scatter_dimension=1, tiled=True)  21.4 us
    pmax x1, blocking collectives, local(): global_top = lax.pmax(row_top, 'slab')  18.7 us
    unnamed x7, waiting for transfers between devices  15.2 us
    unnamed x19, local copies, waits for them, and re-layouts  12.4 us
    dot_general x2, matrix products, local(): jnp.einsum('hrk,khd->hrd', raw_weights.astype(jnp.bfloat16), value_heads,...  11.8 us
    all_gather x1, waiting for transfers between devices, local(): lax.all_gather(finished_keys, ('slab', 'seq'), axis=0, tiled=True)  10.7 us
  transfers between devices with their start and end apart: 6, of which 5 were waited for; matrix products, arithmetic and copies ran while one was open for 16% of the time, Pallas kernels for 0%

commit v1 on v0

--- a/solution.py
+++ b/solution.py
@@ -7,6 +7,20 @@
 HEADS = 40
 HD = 128
 EPSILON = 1e-06
+
+
+def work_both_ways(shard, axis, dim, make, out_dim):
+    ways, here, step = (lax.axis_size(axis), lax.axis_index(axis), shard.shape[dim])
+    earlier, later = ([], [])
+    going_up = going_down = shard
+    for far in range(ways // 2 + 1):
+        earlier.append(make(going_up, (here - far) % ways * step))
+        if 0 < far < ways - ways // 2:
+            later.append(make(going_down, (here + far) % ways * step))
+        going_up = lax.ppermute(going_up, axis, [(d, (d + 1) % ways) for d in range(ways)])
+        going_down = lax.ppermute(going_down, axis, [(d, (d - 1) % ways) for d in range(ways)])
+    line = jnp.concatenate([*earlier[::-1], *later], axis=out_dim)
+    return jnp.roll(line, (here - ways // 2) * earlier[0].shape[out_dim], axis=out_dim)
 
 
 def local(
@@ -78,10 +92,15 @@
         lax.psum_scatter(row_mass * factor, "slab", scatter_dimension=1, tiled=True),
     )
     row_share = (sum_share / mass_share[:, :, None]).astype(jnp.bfloat16)
-    attended = lax.all_gather(row_share, "slab", axis=1, tiled=True)
     weight_heads = out_weight.reshape(head_count, HD, out_weight.shape[1])
-    projected = jnp.einsum(
-        "hrd,hdc->rc", attended, weight_heads, preferred_element_type=jnp.float32
+    projected = work_both_ways(
+        row_share,
+        "slab",
+        1,
+        lambda part, offset: jnp.einsum(
+            "hrd,hdc->rc", part, weight_heads, preferred_element_type=jnp.float32
+        ),
+        0,
     )
     summed = lax.psum_scatter(projected, "head", scatter_dimension=1, tiled=True)
     half = time_weight.shape[0] // 2

time: 241 us -> 234 us (0.971)
  waiting for transfers between devices: 131 us -> 117 us
  starting transfers between devices: 0.2 us -> 4.53 us
  matrix products: 25.7 us -> 28.7 us
    all_gather x1 -> x0, waiting for transfers between devices: 32.2 us -> none  [local(): attended = lax.all_gather(row_share, 'slab', axis=1, tiled=True)]
    ppermute x0 -> x3, waiting for transfers between devices: none -> 19.3 us  [the longest x2 19.3 us: work_both_ways(): lax.ppermute(going_up, axis, [(d, (d + 1) % ways) for d in range(ways)])]
    ppermute x0 -> x3, starting transfers between devices: none -> 4.36 us  [the longest x1 3.82 us: work_both_ways(): lax.ppermute(going_down, axis, [(d, (d - 1) % ways) for d in range(ways)])]
    dot_general x1 -> x4, matrix products: 6.19 us -> 9.12 us  [local(): jnp.einsum('hrd,hdc->rc', part, weight_heads, preferred_element_type=jnp....]
    unnamed x7 -> x6, waiting for transfers between devices: 15.2 us -> 15 us
    unnamed x19 -> x26, local copies, waits for them, and re-layouts: 12.4 us -> 12.5 us
  transfers between devices with their start and end apart: 6 -> 8, of which waited for: 5 -> 6; matrix products, arithmetic and copies ran while one was open for 16% -> 20% of each run, Pallas kernels for 0% -> 0%
where the time goes in v1:
time: 234 us
  waiting for transfers between devices  117 us (50%)
  blocking collectives  29.2 us (12%)
  matrix products  28.7 us (12%)
  local copies, waits for them, and re-layouts  24.8 us (11%)
  between operations  14.7 us (6%)
  other arithmetic  14.5 us (6%)
  starting transfers between devices  4.53 us (2%)
    reduce_scatter x1, waiting for transfers between devices, local(): lax.psum_scatter(partial_value * factor[:, :, None], 'slab', scatter_dime...  51.8 us
    reduce_scatter x1, waiting for transfers between devices, local(): lax.psum_scatter(projected, 'head', scatter_dimension=1, tiled=True)  20.4 us
    ppermute x2, waiting for transfers between devices, work_both_ways(): lax.ppermute(going_up, axis, [(d, (d + 1) % ways) for d in range(ways)])  19.3 us
    pmax x1, blocking collectives, local(): global_top = lax.pmax(row_top, 'slab')  18.7 us
    unnamed x6, waiting for transfers between devices  15 us
    unnamed x26, local copies, waits for them, and re-layouts  12.5 us
    dot_general x2, matrix products, local(): jnp.einsum('hrk,khd->hrd', raw_weights.astype(jnp.bfloat16), value_heads,...  11.9 us
    all_gather x1, waiting for transfers between devices, local(): lax.all_gather(finished_keys, ('slab', 'seq'), axis=0, tiled=True)  10.7 us
  transfers between devices with their start and end apart: 8, of which 6 were waited for; matrix products, arithmetic and copies ran while one was open for 20% of the time, Pallas kernels for 0%

profile of v1, /device:TPU:0, one launch (start us, length us, event | category | flops | bytes accessed | tf_op | source)
XLA Modules:
  0.0 233.6 jit_solution(7393033937256761838)
XLA Ops:
  6.5 0.7 all-gather.3.cloned.1.call-update
  7.3 0.0 all-gather.5.cloned.1.call-start
  7.3 0.7 all-gather.5.cloned.1.call-update
  8.0 0.0 reduce-scatter.10.cloned.1.call-start
  8.1 4.6 %copy.41 = bf16[512,2560]{0,1:T(8,128)(2,1)} copy(bf16[512,2560]{1,0:T(8,128)(2,1)} %param.15) | data formatting | bytes 5242880 | tf_op args[3]
  13.3 0.6 copy.32
  14.0 4.5 %copy.34 = bf16[512,2560]{0,1:T(8,128)(2,1)} copy(bf16[512,2560]{1,0:T(8,128)(2,1)} %param.14) | data formatting | bytes 5242880 | tf_op args[2]
  18.4 2.7 %all_gather.13 = bf16[128,2560]{1,0:T(8,128)(2,1)S(1)} all-gather(bf16[64,2560]{1,0:T(8,128)(2,1)S(1)} %copy-done.4), channel_id=1, replica_groups=mesh['grp'=2,'slab'=4,'head'=2,'seq'=2] {'seq'}, dimensions={0}, use_global_device_ids=true | all-gather | bytes 983040 | tf_op jit(solution)/shard_map/all_gather | solution.py:56
  21.1 1.1 copy.37
  22.2 2.3 all_gather.15
  24.5 1.1 copy.43
  25.6 0.4 fusion.6
  25.9 5.5 %psum.7 = f32[256]{0:T(256)S(1)} all-reduce(f32[256]{0:T(256)S(1)} %fusion.6), channel_id=1, replica_groups=mesh['grp'=2,'slab'=4,'head'=2,'seq'=2] {'head'}, use_global_device_ids=true, to_apply=%region_1.0 | all-reduce | flops 256 | bytes 2048 | tf_op jit(solution)/shard_map/psum | solution.py:43
  31.5 0.4 fusion.8
  31.9 1.2 copy-done.1
  33.1 1.7 multiply_reduce_fusion.1
  34.7 10.7 %all-gather.3.cloned.1.call-done = bf16[512,2560]{1,0:T(8,128)(2,1)} async-done(((bf16[64,2560]{1,0:T(8,128)(2,1)}), bf16[512,2560]{1,0:T(8,128)(2,1)}) %all-gather.3.cloned.1.call-update) | async-done | bytes 2621456 | tf_op jit(solution)/shard_map/all_gather | solution.py:52
  45.4 4.4 %copy.33 = bf16[512,2560]{0,1:T(8,128)(2,1)} copy(bf16[512,2560]{1,0:T(8,128)(2,1)} %all-gather.3.cloned.1.call-done) | data formatting | bytes 5242880 | tf_op jit(solution)/shard_map/all_gather | solution.py:52
  49.8 2.1 broadcast_select_fusion.1
  52.0 5.7 %multiply_reduce_fusion = (f32[20,256]{1,0:T(8,128)S(1)}, f32[20,256,512]{2,1,0:T(8,128)}) fusion(bf16[256,20,128]{0,2,1:T(8,128)(2,1)S(1)} %bitcast.43, bf16[512,20,128]{0,2,1:T(8,128)(2,1)S(1)} %bitcast.45), kind=kOutput, calls=%fused_computation.1 | convolution fusion | flops 676326400 | bytes 14438400 | tf_op jit(solution)/shard_map/rhd,khd->hrk/dot_general | solution.py:69
  57.6 18.7 %pmax.7 = f32[20,256]{1,0:T(8,128)S(1)} all-reduce(f32[20,256]{1,0:T(8,128)S(1)} %max.9), channel_id=1, replica_groups=mesh['grp'=2,'slab'=4,'head'=2,'seq'=2] {'slab'}, use_global_device_ids=true, to_apply=%region_4.5 | all-reduce | flops 5120 | bytes 40960 | tf_op jit(solution)/shard_map/pmax | solution.py:86
  76.4 5.9 %fusion = f32[20,256]{1,0:T(8,128)S(1)} fusion(f32[20,256,512]{2,1,0:T(8,128)} %get-tuple-element.8, f32[20,256]{1,0:T(8,128)S(1)} %max.9), kind=kLoop, calls=%fused_computation.2 | loop fusion | flops 7859200 | bytes 10526720 | tf_op jit(solution)/shard_map/reduce_sum | solution.py:78
  82.2 0.0 all-gather.5.cloned.1.call-done
  82.3 4.5 %copy.40 = bf16[512,2560]{0,1:T(8,128)(2,1)} copy(bf16[512,2560]{1,0:T(8,128)(2,1)} %all-gather.5.cloned.1.call-done) | data formatting | bytes 5242880 | tf_op jit(solution)/shard_map/all_gather | solution.py:53
  86.7 2.0 broadcast_select_fusion
  88.7 7.7 %fusion.2 = f32[20,256,128]{2,1,0:T(8,128)} fusion(bf16[512,20,128]{0,2,1:T(8,128)(2,1)S(1)} %bitcast.44, f32[20,256,512]{2,1,0:T(8,128)} %get-tuple-element.8, f32[20,256]{1,0:T(8,128)S(1)} %max.9), kind=kOutput, calls=%fused_computation.4 | convolution fusion | flops 678952960 | bytes 15749120 | tf_op jit(solution)/shard_map/hrk,khd->hrd/dot_general | solution.py:80
  96.4 0.5 fusion.9
  96.9 0.8 copy.53
  97.7 0.0 reduce-scatter.10.cloned.1.call-update
  97.7 0.0 reduce-scatter.6.cloned.1.call-start
  97.8 4.2 %add_multiply_fusion = f32[20,256,128]{2,1,0:T(8,128)} fusion(f32[20,256,128]{2,1,0:T(8,128)} %fusion.2, bf16[128,20,128]{0,2,1:T(8,128)(2,1)} %bitcast.46, f32[20,256,128]{1,2,0:T(8,128)S(1)} %get-tuple-element.10, f32[20,256]{1,0:T(8,128)S(1)} %get-tuple-element.6, f32[20,256]{1,0:T(8,128)S(1)} %max.9), kind=kOutput, calls=%fused_computation.12 | convolution fusion | flops 171048960 | bytes 8560640 | tf_op jit(solution)/shard_map/hrk,khd->hrd/dot_general | solution.py:80
  102.0 0.0 reduce-scatter.8.cloned.1.call-start
  102.0 13.5 %reduce-scatter.10.cloned.1.call-done = f32[64,20]{1,0:T(8,128)} async-done(((f32[256,20]{1,0:T(8,128)}), f32[64,20]{1,0:T(8,128)}) %reduce-scatter.10.cloned.1.call-update) | async-done | bytes 5136
  115.6 0.8 copy.54
  116.4 51.8 %reduce-scatter.6.cloned.1.call-done = f32[20,64,128]{2,1,0:T(8,128)} async-done(((f32[20,256,128]{2,1,0:T(8,128)}), f32[20,64,128]{2,1,0:T(8,128)}) %reduce-scatter.6.cloned.1.call-update) | async-done | bytes 655376 | tf_op jit(solution)/shard_map/reduce_scatter | solution.py:89
  168.2 1.3 divide_convert_fusion
  169.5 0.5 collective-permute-start
  170.1 10.5 %collective-permute-done = bf16[20,64,128]{2,1,0:T(8,128)(2,1)} collective-permute-done((bf16[20,64,128]{2,1,0:T(8,128)(2,1)S(1)}, bf16[20,64,128]{2,1,0:T(8,128)(2,1)}, u32[]{:S(2)}, u32[]{:S(2)}) %collective-permute-start) | collective-permute-done | bytes 327712 | tf_op jit(solution)/shard_map/ppermute | solution.py:20
  180.5 3.8 %collective-permute-start.2 = (bf16[20,64,128]{2,1,0:T(8,128)(2,1)S(1)}, bf16[20,64,128]{2,1,0:T(8,128)(2,1)S(1)}, u32[]{:S(2)}, u32[]{:S(2)}) collective-permute-start(bf16[20,64,128]{2,1,0:T(8,128)(2,1)S(1)} %divide_convert_fusion), channel_id=1, source_target_pairs={{0,12},{4,0},{8,4},{12,8},{1,13},{5,1},{9,5},{13,9},{2,14},{6,2},{... | collective-permute-start | bytes 983048 | tf_op jit(solution)/shard_map/ppermute | solution.py:21
  184.3 8.9 %collective-permute-done.1 = bf16[20,64,128]{2,1,0:T(8,128)(2,1)} collective-permute-done((bf16[20,64,128]{2,1,0:T(8,128)(2,1)}, bf16[20,64,128]{2,1,0:T(8,128)(2,1)}, u32[]{:S(2)}, u32[]{:S(2)}) %collective-permute-start.1) | collective-permute-done | bytes 327712 | tf_op jit(solution)/shard_map/ppermute | solution.py:20
  193.2 4.4 %constant_dynamic-update-slice_fusion.7 = (f32[512,1280]{1,0:T(8,128)S(1)}, f32[64,1280]{1,0:T(8,128)S(1)}) fusion(bf16[20,64,128]{2,1,0:T(8,128)(2,1)} %collective-permute-done.1, bf16[20,128,1280]{2,1,0:T(8,128)(2,1)} %bitcast.36), kind=kOutput, calls=%fused_computation.37 | convolution fusion | flops 419430400 | bytes 7536640 | tf_op jit(solution)/shard_map/hrd,hdc->rc/dot_general | solution.py:100
  197.6 2.2 constant_dynamic-update-slice_fusion.6
  199.8 1.3 constant_dynamic-update-slice_fusion.5
  201.1 1.3 constant_dynamic-update-slice_fusion.4
  202.5 1.2 constant_dynamic-slice_fusion
  204.4 0.4 convolution_reduce_fusion
  204.9 20.4 %reduce-scatter.8.cloned.1.call-done = f32[256,640]{1,0:T(8,128)} async-done(((f32[256,1280]{1,0:T(8,128)}), f32[256,640]{1,0:T(8,128)}) %reduce-scatter.8.cloned.1.call-update) | async-done | bytes 655376 | tf_op jit(solution)/shard_map/reduce_scatter | solution.py:105
  225.2 1.9 multiply_convert_fusion
  (33 shorter events, 0.3 us)
Async XLA Ops:
  6.5 197.9 %copy-start = (f32[256,640]{1,0:T(8,128)S(1)}, f32[256,640]{1,0:T(8,128)}, u32[]{:S(2)}) copy-start(f32[256,640]{1,0:T(8,128)} %param.21) | copy-start | bytes 1966084
  6.5 38.9 %all-gather.3.cloned.1.call-start = ((), (), s32[]{:S(2)}) async-start(), calls=%async_computation.3 | async-start | bytes 2949120 | tf_op jit(solution)/shard_map/all_gather | solution.py:52
  7.3 75.0 %all-gather.5.cloned.1.call-start = ((), (), s32[]{:S(2)}) async-start(), calls=%async_computation.4 | async-start | bytes 2949120 | tf_op jit(solution)/shard_map/all_gather | solution.py:53
  8.0 107.5 %reduce-scatter.10.cloned.1.call-start = ((), (), s32[]{:S(2)}) async-start(), calls=%async_computation.7 | async-start | bytes 163840
  8.1 5.2 %copy-start.3 = (bf16[256,2560]{1,0:T(8,128)(2,1)S(1)}, bf16[256,2560]{1,0:T(8,128)(2,1)}, u32[]{:S(2)}) copy-start(bf16[256,2560]{1,0:T(8,128)(2,1)} %param.12) | copy-start | bytes 3932164
  13.9 4.5 %copy-start.4 = (bf16[64,2560]{1,0:T(8,128)(2,1)S(1)}, bf16[64,2560]{1,0:T(8,128)(2,1)}, u32[]{:S(2)}) copy-start(bf16[64,2560]{1,0:T(8,128)(2,1)} %param.18) | copy-start | bytes 983044
  13.9 8.3 %copy-start.5 = (bf16[64,2560]{1,0:T(8,128)(2,1)S(1)}, bf16[64,2560]{1,0:T(8,128)(2,1)}, u32[]{:S(2)}) copy-start(bf16[64,2560]{1,0:T(8,128)(2,1)} %param.19) | copy-start | bytes 983044
  21.1 10.4 %copy-start.6 = (f32[2560]{0:T(1024)S(1)}, f32[2560]{0:T(1024)}, u32[]{:S(2)}) copy-start(f32[2560]{0:T(1024)} %param.13) | copy-start | bytes 30724
  31.9 1.2 copy-start.1
  49.8 2.1 copy-start.2
  97.7 70.5 %reduce-scatter.6.cloned.1.call-start = ((), (), s32[]{:S(2)}) async-start(), calls=%async_computation.5 | async-start | bytes 3276800 | tf_op jit(solution)/shard_map/reduce_scatter | solution.py:89
  101.9 95.6 %slice-start = ((s8[6553600]{0:T(1024)(128)(4,1)}), s8[2359296]{0:T(1024)(128)(4,1)S(1)}, s32[]{:S(2)}) async-start(s8[6553600]{0:T(1024)(128)(4,1)} %bitcast.37), calls=%async_computation.8 | async-start | bytes 4718592
  102.0 123.3 %reduce-scatter.8.cloned.1.call-start = ((), (), s32[]{:S(2)}) async-start(), calls=%async_computation.6 | async-start | bytes 1966080 | tf_op jit(solution)/shard_map/reduce_scatter | solution.py:105
  169.5 11.0 %collective-permute-start = (bf16[20,64,128]{2,1,0:T(8,128)(2,1)S(1)}, bf16[20,64,128]{2,1,0:T(8,128)(2,1)}, u32[]{:S(2)}, u32[]{:S(2)}) collective-permute-start(bf16[20,64,128]{2,1,0:T(8,128)(2,1)S(1)} %divide_convert_fusion), channel_id=1, source_target_pairs={{0,4},{4,8},{8,12},{12,0},{1,5},{5,9},{9,13},{13,1},{2,6},{6,10},{... | collective-permute-start | bytes 983048 | tf_op jit(solution)/shard_map/ppermute | solution.py:20
  180.5 12.7 %collective-permute-start.1 = (bf16[20,64,128]{2,1,0:T(8,128)(2,1)}, bf16[20,64,128]{2,1,0:T(8,128)(2,1)}, u32[]{:S(2)}, u32[]{:S(2)}) collective-permute-start(bf16[20,64,128]{2,1,0:T(8,128)(2,1)} %collective-permute-done), channel_id=1, source_target_pairs={{0,4},{4,8},{8,12},{12,0},{1,5},{5,9},{9,13},{13,1},{2,6},{6,10},{... | collective-permute-start | bytes 983048 | tf_op jit(solution)/shard_map/ppermute | solution.py:20
  180.5 20.6 %collective-permute-start.2 = (bf16[20,64,128]{2,1,0:T(8,128)(2,1)S(1)}, bf16[20,64,128]{2,1,0:T(8,128)(2,1)S(1)}, u32[]{:S(2)}, u32[]{:S(2)}) collective-permute-start(bf16[20,64,128]{2,1,0:T(8,128)(2,1)S(1)} %divide_convert_fusion), channel_id=1, source_target_pairs={{0,12},{4,0},{8,4},{12,8},{1,13},{5,1},{9,5},{13,9},{2,14},{6,2},{... | collective-permute-start | bytes 983048 | tf_op jit(solution)/shard_map/ppermute | solution.py:21
  193.2 4.4 %slice-start.1 = ((s8[6553600]{0:T(1024)(128)(4,1)}), s8[4194304]{0:T(1024)(128)(4,1)S(1)}, s32[]{:S(2)}) async-start(s8[6553600]{0:T(1024)(128)(4,1)} %bitcast.37), calls=%async_computation.9 | async-start | bytes 8388608
Sparse Core Ops, SparseCore 0:
  9.0 36.4 all-gather.2
  47.1 33.8 all-gather.4
  97.8 17.6 reduce-scatter.9
  117.7 50.4 reduce-scatter.5
  203.8 21.3 reduce-scatter.7
